TPU v7x, 256 devices: a whole 4x4x8 slice. The times are simulated.
256 devices in a mesh: ctx: 8 (over y, z_lo), exp: 16 (over z_hi, x), rep: 2 (over core).
Axes of the slice: x: 4, y: 4, z: 8 (z_hi: 4, z_lo: 2; z = z_hi * 2 + z_lo), core: 2. Of those that a mesh axis runs over, the one named last changes fastest.
Arguments:
- hidden_in: bfloat16 [8192, 4096], P(('rep', 'ctx', 'exp')), parts along dimension 0, may hold values from -6 to 6
- queries: bfloat16 [8192, 8192], P(('rep', 'ctx'), 'exp'), parts along dimension 0, may hold values from -64 to 64
- keys: bfloat16 [8192, 512], P(('rep', 'ctx')), parts along dimension 0, may hold values from -8 to 8
- values: bfloat16 [8192, 512], P(('rep', 'ctx')), parts along dimension 0, may hold values from -6 to 6
- out_proj: bfloat16 [8192, 4096], P('exp'), may hold values from -0.0625 to 0.0625
- norm_gain: float32 [4096], replicated, may hold values from 0.1 to 1.9
- expert_ids: int32 [8192, 8], P(('rep', 'ctx', 'exp')), parts along dimension 0, may hold values from 0 to 127, all different within a row; in each aligned block of 32 rows (0 to 31, 32 to 63, ...) at most 2 rows name the same one
- gate_fixed: int32 [8192, 8], P(('rep', 'ctx', 'exp')), parts along dimension 0, may hold values from 1 to 4096
- live_counts: int32 [256], P(('rep', 'ctx', 'exp')), parts along dimension 0, may hold values from 16 to 32, as said below
- gate_proj: bfloat16 [16, 4096, 1536], P('exp', None, 'ctx'), may hold values from -0.09375 to 0.09375
- up_proj: bfloat16 [16, 4096, 1536], P('exp', None, 'ctx'), may hold values from -0.09375 to 0.09375
- down_proj: bfloat16 [16, 1536, 4096], P('exp', 'ctx'), may hold values from -0.4375 to 0.4375
Outputs:
- mixed: bfloat16 [8192, 4096], P(('rep', 'ctx', 'exp')), parts along dimension 0
- expert_sum: bfloat16 [8192, 4096], P(('rep', 'ctx', 'exp')), parts along dimension 0
There are 2 independent parts, one for each index of `rep`. A program takes and returns all parts, laid end to end along the dimension named above; an argument that names none is the same for every part. Nothing has to cross between parts.
Inputs may be any that keep to these rules, and one draw needn't show every extreme that they name: `expert_ids`: each row names 8 different experts; among the 32 rows of one device no expert is named by more than 2 rows. `live_counts`: some device has all of its rows live.
All inputs are finite; a program needn't handle non-finite values.
Results may differ from a plain program's by a relative error of at most 0.023.
Values may be sent and summed in bfloat16 or wider, within the bound.
No kernel may reach another device: no remote copies, remote signals or barrier semaphores. Data moves between devices by JAX's collectives and lax.ppermute only.
A program may use at most 64 MiB of HBM per device.

v0:
```python
import jax
import jax.numpy as jnp
from jax import lax
from jax.sharding import PartitionSpec as P

D = 4096
HEADS = 64
KV_HEADS = 4
HEAD_DIM = 128
TOPK = 8
CAP = 2


def on_device(
    hidden_in,
    queries,
    keys,
    values,
    out_proj,
    norm_gain,
    expert_ids,
    gate_fixed,
    live_counts,
    gate_proj,
    up_proj,
    down_proj,
):
    n_ctx = lax.axis_size("ctx")
    n_exp = lax.axis_size("exp")
    seq_rows = queries.shape[0]
    local_heads = queries.shape[1] // HEAD_DIM
    group = HEADS // KV_HEADS
    kv_index = lax.axis_index("exp") * local_heads // group
    key_head = lax.dynamic_slice_in_dim(keys, kv_index * HEAD_DIM, HEAD_DIM, 1)
    value_head = lax.dynamic_slice_in_dim(values, kv_index * HEAD_DIM, HEAD_DIM, 1)
    query_heads = queries.reshape(seq_rows, local_heads, HEAD_DIM).transpose(1, 0, 2)
    query_pos = lax.axis_index("ctx") * seq_rows + jnp.arange(seq_rows, dtype=jnp.int32)
    scale = HEAD_DIM ** (-0.5)

    def update(carry, key_block, value_block, first):
        running, total, accum = carry
        scores = (
            jnp.einsum("hqd,kd->hqk", query_heads, key_block, preferred_element_type=jnp.float32)
            * scale
        )
        key_pos = first + jnp.arange(seq_rows, dtype=jnp.int32)
        visible = (key_pos[None, :] <= query_pos[:, None])[None]
        scores = jnp.where(visible, scores, -1e30)
        newest = jnp.maximum(running, jnp.max(scores, axis=2))
        weights = jnp.where(visible, jnp.exp(scores - newest[..., None]), 0.0)
        factor = jnp.exp(running - newest)
        total = total * factor + jnp.sum(weights, axis=2)
        accum = accum * factor[..., None] + jnp.einsum(
            "hqk,kd->hqd",
            weights.astype(jnp.bfloat16),
            value_block,
            preferred_element_type=jnp.float32,
        )
        return (newest, total, accum)

    start_state = (
        jnp.full((local_heads, seq_rows), -1e30, jnp.float32),
        jnp.zeros((local_heads, seq_rows), jnp.float32),
        jnp.zeros((local_heads, seq_rows, HEAD_DIM), jnp.float32),
    )
    carry = start_state
    key_piece = lax.all_gather(key_head, "ctx", axis=0, tiled=True)
    value_piece = lax.all_gather(value_head, "ctx", axis=0, tiled=True)
    blocks = key_piece.shape[0] // seq_rows
    key_blocks = key_piece.reshape(blocks, seq_rows, HEAD_DIM)
    value_blocks = value_piece.reshape(blocks, seq_rows, HEAD_DIM)
    firsts = jnp.arange(blocks, dtype=jnp.int32) * seq_rows

    def step(state, inputs):
        key_block, value_block, first = inputs
        state = update(state, key_block, value_block, first)
        return (state, None)

    carry, _ = lax.scan(step, carry, (key_blocks, value_blocks, firsts))
    running, total, accum = carry
    attended = (
        (accum / total[..., None])
        .astype(jnp.bfloat16)
        .transpose(1, 0, 2)
        .reshape(seq_rows, local_heads * HEAD_DIM)
    )
    token_rows = hidden_in.shape[0]
    attn_out = lax.psum_scatter(
        jnp.dot(attended, out_proj, preferred_element_type=jnp.float32).astype(jnp.bfloat16),
        "exp",
        scatter_dimension=0,
        tiled=True,
    ).astype(jnp.float32)
    residual = hidden_in.astype(jnp.float32) + attn_out
    mixed = residual.astype(jnp.bfloat16)
    norm_scale = lax.rsqrt(jnp.mean(residual * residual, axis=1, keepdims=True) + 1e-06)
    normed = (residual * norm_scale * norm_gain).astype(jnp.bfloat16)
    slot_count = n_exp * CAP
    live = jnp.arange(token_rows, dtype=jnp.int32) < live_counts[0]
    active = (expert_ids < n_exp) & live[:, None]
    onehot = (
        (expert_ids[..., None] == jnp.arange(n_exp, dtype=jnp.int32)) & active[..., None]
    ).astype(jnp.int32)
    onehot = onehot.reshape(token_rows * TOPK, n_exp)
    earlier = jnp.cumsum(onehot, axis=0) - onehot
    rank = jnp.sum(earlier * onehot, axis=1).reshape(token_rows, TOPK)
    slot = jnp.where(active, expert_ids * CAP + rank, -1)
    pair_hit = slot[..., None] == jnp.arange(slot_count, dtype=jnp.int32)
    dispatch = jnp.any(pair_hit, axis=1).astype(jnp.bfloat16)
    send = jnp.einsum("rs,rd->sd", dispatch, normed, preferred_element_type=jnp.float32).astype(
        jnp.bfloat16
    )
    send = send.reshape(n_exp, CAP, D)
    route_weights = gate_fixed.astype(jnp.float32) / 4096.0
    combine = jnp.sum(pair_hit.astype(jnp.float32) * route_weights[..., None], axis=1)
    copies = jnp.broadcast_to(send[None], (n_ctx, n_exp, CAP, D)).reshape(n_ctx * n_exp, CAP, D)
    rows3 = lax.all_to_all(copies, ("ctx", "exp"), split_axis=0, concat_axis=0, tiled=True)
    flat_rows = rows3.reshape(-1, D)
    gate_part = jnp.dot(flat_rows, gate_proj[0], preferred_element_type=jnp.float32)
    up_part = jnp.dot(flat_rows, up_proj[0], preferred_element_type=jnp.float32)
    hidden = (jax.nn.silu(gate_part) * up_part).astype(jnp.bfloat16)
    partial_value = jnp.dot(hidden, down_proj[0], preferred_element_type=jnp.float32)
    partial_value = partial_value.reshape(rows3.shape[0], rows3.shape[1], D).astype(jnp.bfloat16)
    returned = lax.all_to_all(
        partial_value, ("ctx", "exp"), split_axis=0, concat_axis=0, tiled=True
    )
    expert_out = (
        returned.astype(jnp.float32).reshape(n_ctx, slot_count, D).sum(axis=0).astype(jnp.bfloat16)
    )
    expert_sum = jnp.dot(combine, expert_out.astype(jnp.float32), precision=lax.Precision.HIGHEST)
    return (mixed, expert_sum.astype(jnp.bfloat16))


def solution(mesh):
    in_specs = (
        P(("rep", "ctx", "exp"), None),
        P(("rep", "ctx"), "exp"),
        P(("rep", "ctx"), None),
        P(("rep", "ctx"), None),
        P("exp", None),
        P(),
        P(("rep", "ctx", "exp"), None),
        P(("rep", "ctx", "exp"), None),
        P(("rep", "ctx", "exp")),
        P("exp", None, "ctx"),
        P("exp", None, "ctx"),
        P("exp", "ctx", None),
    )
    out_specs = (P(("rep", "ctx", "exp"), None), P(("rep", "ctx", "exp"), None))
    return jax.shard_map(
        on_device, mesh=mesh, in_specs=in_specs, out_specs=out_specs, check_vma=False
    )
```

profile of v0, /device:TPU:64, one launch (start us, length us, event | category | flops | bytes accessed | tf_op | source)
XLA Modules:
  0.0 457.7 jit_solution(1210172698889403102)
XLA Ops:
  12.2 43.5 %all-gather.3.cloned.1.call-done = bf16[4096,128]{1,0:T(8,128)(2,1)} async-done(((bf16[512,128]{1,0:T(8,128)(2,1)}), bf16[4096,128]{1,0:T(8,128)(2,1)}) %all-gather.3.cloned.1.call-update) | async-done | bytes 1048592 | tf_op jit(solution)/shard_map/all_gather | solution.py:67
  55.7 44.4 %all-gather.5.cloned.1.call-done = bf16[4096,128]{1,0:T(8,128)(2,1)} async-done(((bf16[512,128]{1,0:T(8,128)(2,1)}), bf16[4096,128]{1,0:T(8,128)(2,1)}) %all-gather.5.cloned.1.call-update) | async-done | bytes 1048592 | tf_op jit(solution)/shard_map/all_gather | solution.py:68
  100.1 100.9 %while.15 = (s32[]{:T(128)}, f32[4,512]{1,0:T(4,128)S(1)}, f32[4,512]{1,0:T(4,128)S(1)}, f32[4,512,128]{2,1,0:T(8,128)}, s32[8]{0:T(128)S(1)}, /*index=5*/bf16[8...) while((s32[]{:T(128)}, f32[4,512]{1,0:T(4,128)S(1)}, ...), condition=%wide.region_3.4_spmd.clone, body=%wide.region_0.3_spmd.clone.sunk | while | flops 551562240 | bytes 41821408 | solution.py:79
  101.5 3.8 fusion.62
  105.3 3.4 fusion.63
  114.1 3.8 fusion.62
  117.9 3.4 fusion.63
  126.7 3.8 fusion.62
  130.5 3.4 fusion.63
  139.4 3.8 fusion.62
  143.1 3.4 fusion.63
  152.0 3.8 fusion.62
  155.8 3.4 fusion.63
  164.6 3.8 fusion.62
  177.2 3.8 fusion.62
  189.8 3.8 fusion.62
  202.6 6.5 %convolution_convert_fusion = bf16[512,4096]{1,0:T(8,128)(2,1)} fusion(bf16[512,512]{0,1:T(8,128)(2,1)S(1)} %bitcast.91, bf16[512,4096]{1,0:T(8,128)(2,1)} %param.18), kind=kOutput, calls=%fused_computation.27 | convolution fusion | flops 2149580800 | bytes 8912896 | tf_op jit(solution)/shard_map/dot_general | solution.py:89
  212.2 90.7 %reduce-scatter.2.cloned.1.call-done = bf16[32,4096]{1,0:T(8,128)(2,1)} async-done(((bf16[512,4096]{1,0:T(8,128)(2,1)}), bf16[32,4096]{1,0:T(8,128)(2,1)}) %reduce-scatter.2.cloned.1.call-update) | async-done | bytes 262160 | tf_op jit(solution)/shard_map/reduce_scatter | solution.py:88
  308.4 63.4 %all_to_all.10 = bf16[128,2,4096]{2,1,0:T(2,128)(2,1)} all-to-all(bf16[128,2,4096]{2,1,0:T(2,128)(2,1)S(1)} %bitcast.90), channel_id=1, replica_groups=mesh['ctx'=8,'exp'=16,'rep'=2] {'ctx','exp'}, dimensions={0} | all-to-all | bytes 4194304 | tf_op jit(solution)/shard_map/all_to_all | solution.py:117
  371.8 4.1 reshape.115
  382.2 3.5 copy.56
  385.7 6.7 %all-to-all-start.1 = ((bf16[128,2,4096]{2,1,0:T(2,128)(2,1)}), bf16[128,2,4096]{2,1,0:T(2,128)(2,1)}, u32[]{:S(2)}, u32[]{:S(2)}) async-start(bf16[128,2,4096]{2,1,0:T(2,128)(2,1)} %copy.56), calls=%async_computation.2 | async-start | bytes 4194304 | tf_op jit(solution)/shard_map/all_to_all | solution.py:124
  392.6 51.5 %all-to-all-done.1 = bf16[128,2,4096]{2,1,0:T(2,128)(2,1)} async-done(((bf16[128,2,4096]{2,1,0:T(2,128)(2,1)}), bf16[128,2,4096]{2,1,0:T(2,128)(2,1)}, u32[]{:S(2)}, u32[]{:S(2)}) %all-to-all-start.1) | async-done | bytes 2097184 | tf_op jit(solution)/shard_map/all_to_all | solution.py:124
  444.1 4.1 reshape.116
  (166 shorter events, 77.0 us)
Async XLA Ops:
  7.2 374.3 %copy-start = (bf16[1,192,4096]{2,1,0:T(8,128)(2,1)S(1)}, bf16[1,192,4096]{2,1,0:T(8,128)(2,1)}, u32[]{:S(2)}) copy-start(bf16[1,192,4096]{2,1,0:T(8,128)(2,1)} %param.25) | copy-start | bytes 4718596
  7.2 48.5 %all-gather.3.cloned.1.call-start = ((), (), s32[]{:S(2)}) async-start(), calls=%async_computation.3 | async-start | bytes 1179648 | tf_op jit(solution)/shard_map/all_gather | solution.py:67
  8.9 91.1 %all-gather.5.cloned.1.call-start = ((), (), s32[]{:S(2)}) async-start(), calls=%async_computation.4 | async-start | bytes 1179648 | tf_op jit(solution)/shard_map/all_gather | solution.py:68
  10.6 292.4 %reduce-scatter.2.cloned.1.call-start = ((), (), s32[]{:S(2)}) async-start(), calls=%async_computation.5 | async-start | bytes 4456448 | tf_op jit(solution)/shard_map/reduce_scatter | solution.py:88
  101.5 7.2 %copy-start.3 = (f32[4,512,128]{2,1,0:T(8,128)S(1)}, f32[4,512,128]{2,1,0:T(8,128)}, u32[]{:S(2)}) copy-start(f32[4,512,128]{2,1,0:T(8,128)} %get-tuple-element.219) | copy-start | bytes 3145732 | tf_op jit(solution)/shard_map/while
  105.3 3.4 copy-start.1
  114.1 7.2 %copy-start.3 = (f32[4,512,128]{2,1,0:T(8,128)S(1)}, f32[4,512,128]{2,1,0:T(8,128)}, u32[]{:S(2)}) copy-start(f32[4,512,128]{2,1,0:T(8,128)} %get-tuple-element.219) | copy-start | bytes 3145732 | tf_op jit(solution)/shard_map/while
  117.9 3.4 copy-start.1
  126.7 7.2 %copy-start.3 = (f32[4,512,128]{2,1,0:T(8,128)S(1)}, f32[4,512,128]{2,1,0:T(8,128)}, u32[]{:S(2)}) copy-start(f32[4,512,128]{2,1,0:T(8,128)} %get-tuple-element.219) | copy-start | bytes 3145732 | tf_op jit(solution)/shard_map/while
  130.5 3.4 copy-start.1
  139.3 7.2 %copy-start.3 = (f32[4,512,128]{2,1,0:T(8,128)S(1)}, f32[4,512,128]{2,1,0:T(8,128)}, u32[]{:S(2)}) copy-start(f32[4,512,128]{2,1,0:T(8,128)} %get-tuple-element.219) | copy-start | bytes 3145732 | tf_op jit(solution)/shard_map/while
  143.1 3.4 copy-start.1
  152.0 7.2 %copy-start.3 = (f32[4,512,128]{2,1,0:T(8,128)S(1)}, f32[4,512,128]{2,1,0:T(8,128)}, u32[]{:S(2)}) copy-start(f32[4,512,128]{2,1,0:T(8,128)} %get-tuple-element.219) | copy-start | bytes 3145732 | tf_op jit(solution)/shard_map/while
  155.7 3.4 copy-start.1
  164.6 7.2 %copy-start.3 = (f32[4,512,128]{2,1,0:T(8,128)S(1)}, f32[4,512,128]{2,1,0:T(8,128)}, u32[]{:S(2)}) copy-start(f32[4,512,128]{2,1,0:T(8,128)} %get-tuple-element.219) | copy-start | bytes 3145732 | tf_op jit(solution)/shard_map/while
  168.4 3.4 copy-start.1
  177.2 7.2 %copy-start.3 = (f32[4,512,128]{2,1,0:T(8,128)S(1)}, f32[4,512,128]{2,1,0:T(8,128)}, u32[]{:S(2)}) copy-start(f32[4,512,128]{2,1,0:T(8,128)} %get-tuple-element.219) | copy-start | bytes 3145732 | tf_op jit(solution)/shard_map/while
  189.8 7.2 %copy-start.3 = (f32[4,512,128]{2,1,0:T(8,128)S(1)}, f32[4,512,128]{2,1,0:T(8,128)}, u32[]{:S(2)}) copy-start(f32[4,512,128]{2,1,0:T(8,128)} %get-tuple-element.219) | copy-start | bytes 3145732 | tf_op jit(solution)/shard_map/while
  193.6 3.4 copy-start.1
  209.1 93.9 %copy-start.5 = (bf16[32,4096]{1,0:T(8,128)(2,1)S(1)}, bf16[32,4096]{1,0:T(8,128)(2,1)}, u32[]{:S(2)}) copy-start(bf16[32,4096]{1,0:T(8,128)(2,1)} %param.14) | copy-start | bytes 786436
  209.1 95.7 %copy-start.6 = (f32[4096]{0:T(1024)S(1)}, f32[4096]{0:T(1024)}, u32[]{:S(2)}) copy-start(f32[4096]{0:T(1024)} %param.19) | copy-start | bytes 49156
  308.4 67.5 %copy-start.2 = (bf16[1,4096,192]{1,2,0:T(8,128)(2,1)S(1)}, bf16[1,4096,192]{1,2,0:T(8,128)(2,1)}, u32[]{:S(2)}) copy-start(bf16[1,4096,192]{1,2,0:T(8,128)(2,1)} %param.23) | copy-start | bytes 4718596
  382.1 10.2 %copy-start.8 = (s32[32,8]{0,1:T(8,128)S(1)}, s32[32,8]{0,1:T(8,128)}, u32[]{:S(2)}) copy-start(s32[32,8]{0,1:T(8,128)} %param.21) | copy-start | bytes 3076
  385.7 58.4 %all-to-all-start.1 = ((bf16[128,2,4096]{2,1,0:T(2,128)(2,1)}), bf16[128,2,4096]{2,1,0:T(2,128)(2,1)}, u32[]{:S(2)}, u32[]{:S(2)}) async-start(bf16[128,2,4096]{2,1,0:T(2,128)(2,1)} %copy.56), calls=%async_computation.2 | async-start | bytes 4194304 | tf_op jit(solution)/shard_map/all_to_all | solution.py:124
  (10 other events, 12.2 us)
Sparse Core Ops, SparseCore 0:
  10.4 45.2 all-gather.2
  58.0 41.9 all-gather.4
  209.3 93.6 reduce-scatter.1
where the time goes:
time: 459 us; the launch traced here: 458 us
  waiting for transfers between devices  230 us (50%)
  matrix products  68.2 us (15%)
  blocking collectives  63.4 us (14%)
  other arithmetic  39.3 us (9%)
  local copies, waits for them, and re-layouts  34.7 us (8%)
  between operations  14.6 us (3%)
  starting transfers between devices  6.8 us (1%)
    reduce_scatter x1, waiting for transfers between devices, on_device(): lax.psum_scatter(jnp.dot(attended, out_proj, preferred_element_type=jnp.f...  90.7 us
    all_to_all x1, blocking collectives, on_device(): lax.all_to_all(copies, ('ctx', 'exp'), split_axis=0, concat_axis=0, tiled...  63.4 us
    all_to_all x1, waiting for transfers between devices, on_device(): lax.all_to_all(partial_value, ('ctx', 'exp'), split_axis=0, concat_axis=0...  51.5 us
    all_gather x1, waiting for transfers between devices, on_device(): value_piece = lax.all_gather(value_head, 'ctx', axis=0, tiled=True)  44.4 us
    all_gather x1, waiting for transfers between devices, on_device(): key_piece = lax.all_gather(key_head, 'ctx', axis=0, tiled=True)  43.5 us
    dot_general x8, matrix products, update(): jnp.einsum('hqd,kd->hqk', query_heads, key_block, preferred_element_type=...  30.2 us
    reduce_sum x8, other arithmetic, update(): total = total * factor + jnp.sum(weights, axis=2)  27.1 us
    dot_general x8, matrix products, update(): jnp.einsum('hqk,kd->hqd', weights.astype(jnp.bfloat16), value_block, pref...  23.2 us
  transfers between devices with their start and end apart: 4, of which 4 were waited for; matrix products, arithmetic and copies ran while one was open for 1% of the time, Pallas kernels for 0%

commit v1 on v0

--- a/solution.py
+++ b/solution.py
@@ -65,7 +65,9 @@
     )
     carry = start_state
     key_piece = lax.all_gather(key_head, "ctx", axis=0, tiled=True)
-    value_piece = lax.all_gather(value_head, "ctx", axis=0, tiled=True)
+    value_piece = jnp.concatenate(
+        lax.all_to_all(jnp.stack([value_head] * lax.axis_size("ctx")), "ctx", 0, 0), axis=0
+    )
     blocks = key_piece.shape[0] // seq_rows
     key_blocks = key_piece.reshape(blocks, seq_rows, HEAD_DIM)
     value_blocks = value_piece.reshape(blocks, seq_rows, HEAD_DIM)

time: 459 us -> 422 us (0.919)
  waiting for transfers between devices: 230 us -> 188 us
  starting transfers between devices: 6.8 us -> 12.6 us
    all_gather x1 -> x0, waiting for transfers between devices: 44.4 us -> none  [on_device(): value_piece = lax.all_gather(value_head, 'ctx', axis=0, tiled=True)]
    all_to_all x0 -> x1, waiting for transfers between devices: none -> 13.6 us  [on_device(): lax.all_to_all(jnp.stack([value_head] * lax.axis_size('ctx')), 'ctx', 0, 0)]
    all_gather x1, waiting for transfers between devices: 43.5 us -> 32.1 us  [on_device(): key_piece = lax.all_gather(key_head, 'ctx', axis=0, tiled=True)]
    all_to_all x0 -> x1, starting transfers between devices: none -> 5.82 us  [on_device(): lax.all_to_all(jnp.stack([value_head] * lax.axis_size('ctx')), 'ctx', 0, 0)]
where the time goes in v1:
time: 422 us; the launch traced here: 421 us
  waiting for transfers between devices  188 us (45%)
  matrix products  68.2 us (16%)
  blocking collectives  63.5 us (15%)
  other arithmetic  39.3 us (9%)
  local copies, waits for them, and re-layouts  34.2 us (8%)
  between operations  15 us (4%)
  starting transfers between devices  12.6 us (3%)
    reduce_scatter x1, waiting for transfers between devices, on_device(): lax.psum_scatter(jnp.dot(attended, out_proj, preferred_element_type=jnp.f...  90.6 us
    all_to_all x1, blocking collectives, on_device(): lax.all_to_all(copies, ('ctx', 'exp'), split_axis=0, concat_axis=0, tiled...  63.5 us
    all_to_all x1, waiting for transfers between devices, on_device(): lax.all_to_all(partial_value, ('ctx', 'exp'), split_axis=0, concat_axis=0...  51.5 us
    all_gather x1, waiting for transfers between devices, on_device(): key_piece = lax.all_gather(key_head, 'ctx', axis=0, tiled=True)  32.1 us
    dot_general x8, matrix products, update(): jnp.einsum('hqd,kd->hqk', query_heads, key_block, preferred_element_type=...  30.2 us
    reduce_sum x8, other arithmetic, update(): total = total * factor + jnp.sum(weights, axis=2)  27.1 us
    dot_general x8, matrix products, update(): jnp.einsum('hqk,kd->hqd', weights.astype(jnp.bfloat16), value_block, pref...  23.2 us
    all_to_all x1, waiting for transfers between devices, on_device(): lax.all_to_all(jnp.stack([value_head] * lax.axis_size('ctx')), 'ctx', 0, 0)  13.6 us
  transfers between devices with their start and end apart: 4, of which 4 were waited for; matrix products, arithmetic and copies ran while one was open for 1% of the time, Pallas kernels for 0%

profile of v1, /device:TPU:64, one launch (start us, length us, event | category | flops | bytes accessed | tf_op | source)
XLA Modules:
  0.0 421.1 jit_solution(540834273336825997)
XLA Ops:
  9.4 5.8 %all-to-all-start = ((bf16[8,512,128]{2,1,0:T(8,128)(2,1)}), bf16[8,512,128]{2,1,0:T(8,128)(2,1)}, u32[]{:S(2)}, u32[]{:S(2)}) async-start(bf16[8,512,128]{2,1,0:T(8,128)(2,1)} %stack.2), calls=%async_computation | async-start | bytes 2097152 | tf_op jit(solution)/shard_map/all_to_all | solution.py:69
  17.5 13.6 %all-to-all-done = bf16[8,512,128]{2,1,0:T(8,128)(2,1)} async-done(((bf16[8,512,128]{2,1,0:T(8,128)(2,1)}), bf16[8,512,128]{2,1,0:T(8,128)(2,1)}, u32[]{:S(2)}, u32[]{:S(2)}) %all-to-all-start) | async-done | bytes 1048608 | tf_op jit(solution)/shard_map/all_to_all | solution.py:69
  31.0 32.1 %all-gather.2.cloned.1.call-done = bf16[4096,128]{1,0:T(8,128)(2,1)} async-done(((bf16[512,128]{1,0:T(8,128)(2,1)}), bf16[4096,128]{1,0:T(8,128)(2,1)}) %all-gather.2.cloned.1.call-update) | async-done | bytes 1048592 | tf_op jit(solution)/shard_map/all_gather | solution.py:67
  63.2 100.9 %while.15 = (s32[]{:T(128)}, f32[4,512]{1,0:T(4,128)S(1)}, f32[4,512]{1,0:T(4,128)S(1)}, f32[4,512,128]{2,1,0:T(8,128)}, s32[8]{0:T(128)S(1)}, /*index=5*/bf16[8...) while((s32[]{:T(128)}, f32[4,512]{1,0:T(4,128)S(1)}, ...), condition=%wide.region_3.4_spmd.clone, body=%wide.region_0.3_spmd.clone.sunk | while | flops 551562240 | bytes 41821408 | solution.py:81
  64.6 3.8 fusion.62
  68.4 3.4 fusion.63
  77.2 3.8 fusion.62
  81.0 3.4 fusion.63
  89.8 3.8 fusion.62
  93.6 3.4 fusion.63
  102.5 3.8 fusion.62
  106.2 3.4 fusion.63
  115.1 3.8 fusion.62
  127.7 3.8 fusion.62
  140.3 3.8 fusion.62
  152.9 3.8 fusion.62
  165.7 6.5 %convolution_convert_fusion = bf16[512,4096]{1,0:T(8,128)(2,1)} fusion(bf16[512,512]{0,1:T(8,128)(2,1)S(1)} %bitcast.90, bf16[512,4096]{1,0:T(8,128)(2,1)} %param.18), kind=kOutput, calls=%fused_computation.27 | convolution fusion | flops 2149580800 | bytes 8912896 | tf_op jit(solution)/shard_map/dot_general | solution.py:91
  175.3 90.6 %reduce-scatter.2.cloned.1.call-done = bf16[32,4096]{1,0:T(8,128)(2,1)} async-done(((bf16[512,4096]{1,0:T(8,128)(2,1)}), bf16[32,4096]{1,0:T(8,128)(2,1)}) %reduce-scatter.2.cloned.1.call-update) | async-done | bytes 262160 | tf_op jit(solution)/shard_map/reduce_scatter | solution.py:90
  271.3 63.5 %all_to_all.15 = bf16[128,2,4096]{2,1,0:T(2,128)(2,1)} all-to-all(bf16[128,2,4096]{2,1,0:T(2,128)(2,1)S(1)} %bitcast.89), channel_id=1, replica_groups=mesh['ctx'=8,'exp'=16,'rep'=2] {'ctx','exp'}, dimensions={0} | all-to-all | bytes 4194304 | tf_op jit(solution)/shard_map/all_to_all | solution.py:119
  334.8 4.1 reshape.113
  345.2 3.5 copy.56
  348.7 6.7 %all-to-all-start.2 = ((bf16[128,2,4096]{2,1,0:T(2,128)(2,1)}), bf16[128,2,4096]{2,1,0:T(2,128)(2,1)}, u32[]{:S(2)}, u32[]{:S(2)}) async-start(bf16[128,2,4096]{2,1,0:T(2,128)(2,1)} %copy.56), calls=%async_computation.3 | async-start | bytes 4194304 | tf_op jit(solution)/shard_map/all_to_all | solution.py:126
  355.6 51.5 %all-to-all-done.2 = bf16[128,2,4096]{2,1,0:T(2,128)(2,1)} async-done(((bf16[128,2,4096]{2,1,0:T(2,128)(2,1)}), bf16[128,2,4096]{2,1,0:T(2,128)(2,1)}, u32[]{:S(2)}, u32[]{:S(2)}) %all-to-all-start.2) | async-done | bytes 2097184 | tf_op jit(solution)/shard_map/all_to_all | solution.py:126
  407.2 4.1 reshape.114
  (168 shorter events, 79.8 us)
Async XLA Ops:
  7.2 337.3 %copy-start = (bf16[1,192,4096]{2,1,0:T(8,128)(2,1)S(1)}, bf16[1,192,4096]{2,1,0:T(8,128)(2,1)}, u32[]{:S(2)}) copy-start(bf16[1,192,4096]{2,1,0:T(8,128)(2,1)} %param.25) | copy-start | bytes 4718596
  7.2 9.8 %copy-start.6 = (bf16[512,512]{1,0:T(8,128)(2,1)S(1)}, bf16[512,512]{1,0:T(8,128)(2,1)}, u32[]{:S(2)}) copy-start(bf16[512,512]{1,0:T(8,128)(2,1)} %param.15) | copy-start | bytes 1572868
  9.4 21.6 %all-to-all-start = ((bf16[8,512,128]{2,1,0:T(8,128)(2,1)}), bf16[8,512,128]{2,1,0:T(8,128)(2,1)}, u32[]{:S(2)}, u32[]{:S(2)}) async-start(bf16[8,512,128]{2,1,0:T(8,128)(2,1)} %stack.2), calls=%async_computation | async-start | bytes 2097152 | tf_op jit(solution)/shard_map/all_to_all | solution.py:69
  15.2 47.9 %all-gather.2.cloned.1.call-start = ((), (), s32[]{:S(2)}) async-start(), calls=%async_computation.4 | async-start | bytes 1179648 | tf_op jit(solution)/shard_map/all_gather | solution.py:67
  16.9 249.0 %reduce-scatter.2.cloned.1.call-start = ((), (), s32[]{:S(2)}) async-start(), calls=%async_computation.5 | async-start | bytes 4456448 | tf_op jit(solution)/shard_map/reduce_scatter | solution.py:90
  64.6 7.2 %copy-start.3 = (f32[4,512,128]{2,1,0:T(8,128)S(1)}, f32[4,512,128]{2,1,0:T(8,128)}, u32[]{:S(2)}) copy-start(f32[4,512,128]{2,1,0:T(8,128)} %get-tuple-element.219) | copy-start | bytes 3145732 | tf_op jit(solution)/shard_map/while
  68.4 3.4 copy-start.1
  77.2 7.2 %copy-start.3 = (f32[4,512,128]{2,1,0:T(8,128)S(1)}, f32[4,512,128]{2,1,0:T(8,128)}, u32[]{:S(2)}) copy-start(f32[4,512,128]{2,1,0:T(8,128)} %get-tuple-element.219) | copy-start | bytes 3145732 | tf_op jit(solution)/shard_map/while
  81.0 3.4 copy-start.1
  89.8 7.2 %copy-start.3 = (f32[4,512,128]{2,1,0:T(8,128)S(1)}, f32[4,512,128]{2,1,0:T(8,128)}, u32[]{:S(2)}) copy-start(f32[4,512,128]{2,1,0:T(8,128)} %get-tuple-element.219) | copy-start | bytes 3145732 | tf_op jit(solution)/shard_map/while
  93.6 3.4 copy-start.1
  102.4 7.2 %copy-start.3 = (f32[4,512,128]{2,1,0:T(8,128)S(1)}, f32[4,512,128]{2,1,0:T(8,128)}, u32[]{:S(2)}) copy-start(f32[4,512,128]{2,1,0:T(8,128)} %get-tuple-element.219) | copy-start | bytes 3145732 | tf_op jit(solution)/shard_map/while
  106.2 3.4 copy-start.1
  115.0 7.2 %copy-start.3 = (f32[4,512,128]{2,1,0:T(8,128)S(1)}, f32[4,512,128]{2,1,0:T(8,128)}, u32[]{:S(2)}) copy-start(f32[4,512,128]{2,1,0:T(8,128)} %get-tuple-element.219) | copy-start | bytes 3145732 | tf_op jit(solution)/shard_map/while
  118.8 3.4 copy-start.1
  127.7 7.2 %copy-start.3 = (f32[4,512,128]{2,1,0:T(8,128)S(1)}, f32[4,512,128]{2,1,0:T(8,128)}, u32[]{:S(2)}) copy-start(f32[4,512,128]{2,1,0:T(8,128)} %get-tuple-element.219) | copy-start | bytes 3145732 | tf_op jit(solution)/shard_map/while
  131.4 3.4 copy-start.1
  140.3 7.2 %copy-start.3 = (f32[4,512,128]{2,1,0:T(8,128)S(1)}, f32[4,512,128]{2,1,0:T(8,128)}, u32[]{:S(2)}) copy-start(f32[4,512,128]{2,1,0:T(8,128)} %get-tuple-element.219) | copy-start | bytes 3145732 | tf_op jit(solution)/shard_map/while
  152.9 7.2 %copy-start.3 = (f32[4,512,128]{2,1,0:T(8,128)S(1)}, f32[4,512,128]{2,1,0:T(8,128)}, u32[]{:S(2)}) copy-start(f32[4,512,128]{2,1,0:T(8,128)} %get-tuple-element.219) | copy-start | bytes 3145732 | tf_op jit(solution)/shard_map/while
  172.2 93.7 %copy-start.5 = (bf16[32,4096]{1,0:T(8,128)(2,1)S(1)}, bf16[32,4096]{1,0:T(8,128)(2,1)}, u32[]{:S(2)}) copy-start(bf16[32,4096]{1,0:T(8,128)(2,1)} %param.14) | copy-start | bytes 786436
  172.2 95.6 %copy-start.7 = (f32[4096]{0:T(1024)S(1)}, f32[4096]{0:T(1024)}, u32[]{:S(2)}) copy-start(f32[4096]{0:T(1024)} %param.19) | copy-start | bytes 49156
  271.3 67.6 %copy-start.2 = (bf16[1,4096,192]{1,2,0:T(8,128)(2,1)S(1)}, bf16[1,4096,192]{1,2,0:T(8,128)(2,1)}, u32[]{:S(2)}) copy-start(bf16[1,4096,192]{1,2,0:T(8,128)(2,1)} %param.23) | copy-start | bytes 4718596
  345.2 10.2 %copy-start.9 = (s32[32,8]{0,1:T(8,128)S(1)}, s32[32,8]{0,1:T(8,128)}, u32[]{:S(2)}) copy-start(s32[32,8]{0,1:T(8,128)} %param.21) | copy-start | bytes 3076
  348.7 58.5 %all-to-all-start.2 = ((bf16[128,2,4096]{2,1,0:T(2,128)(2,1)}), bf16[128,2,4096]{2,1,0:T(2,128)(2,1)}, u32[]{:S(2)}, u32[]{:S(2)}) async-start(bf16[128,2,4096]{2,1,0:T(2,128)(2,1)} %copy.56), calls=%async_computation.3 | async-start | bytes 4194304 | tf_op jit(solution)/shard_map/all_to_all | solution.py:126
  (11 other events, 15.6 us)
Sparse Core Ops, SparseCore 0:
  18.4 44.6 all-gather.1
  172.4 93.4 reduce-scatter.1
